TPU v7x, 32 devices: a whole 2x2x4 slice. The times are simulated.
32 devices in a mesh: wide: 8 (over z, y), narrow: 4 (over x, core).
Axes of the slice: x: 2, y: 2, z: 4, core: 2. Of those that a mesh axis runs over, the one named last changes fastest.
Arguments:
- frames: bfloat16 [256, 2, 256, 256], P(('wide', 'narrow')), may hold values from -120 to 120
- sketch: bfloat16 [256, 128], replicated, may hold values from -0.3 to 2.3
- kernel_taps: bfloat16 [64], replicated, may hold values from -0.3 to 1.1
Outputs:
- basis: float32 [128, 32768], P(None, ('wide', 'narrow'))
- factor: float32 [128, 128], replicated
All inputs are finite; a program needn't handle non-finite values.
Results may differ from a plain program's by a relative error of at most 0.0043.
Values may be sent and summed in bfloat16 or wider, within the bound.
No kernel may reach another device: no remote copies, remote signals or barrier semaphores. Data moves between devices by JAX's collectives and lax.ppermute only.
A program may use at most 64 MiB of HBM per device.

v0:
```python
import jax
import jax.numpy as jnp
from jax import lax
from jax.sharding import PartitionSpec as P


def gauss_taps(spread):
    position = jnp.arange(15, dtype=jnp.float32) - 7.0
    weights = jnp.exp(-position * position / (2.0 * spread * spread))
    return weights / jnp.sum(weights)


def band_matrix(spread, length):
    outputs = length // 2
    offset_index = (
        jnp.arange(length, dtype=jnp.int32)[None, :]
        - 2 * jnp.arange(outputs, dtype=jnp.int32)[:, None]
        + 7
    )
    weights = gauss_taps(spread)
    matrix = jnp.zeros((outputs, length), jnp.float32)
    for offset in range(15):
        matrix = matrix + jnp.where(offset_index == offset, weights[offset], jnp.float32(0.0))
    return matrix


def filter_volumes(frames_block):
    volume = frames_block.astype(jnp.float32)
    row_count = volume.shape[-2]
    col_count = volume.shape[-1]
    half = col_count // 2
    column_bands = jnp.concatenate(
        [band_matrix(1.5, col_count), band_matrix(3.0, col_count)], axis=0
    )
    column_pass = jnp.einsum(
        "...rc,oc->...ro", volume, column_bands, precision=lax.Precision.HIGHEST
    )
    narrow_pass = jnp.einsum(
        "or,...rc->...oc",
        band_matrix(1.5, row_count),
        column_pass[..., :half],
        precision=lax.Precision.HIGHEST,
    )
    broad_pass = jnp.einsum(
        "or,...rc->...oc",
        band_matrix(3.0, row_count),
        column_pass[..., half:],
        precision=lax.Precision.HIGHEST,
    )
    return (narrow_pass - broad_pass).astype(jnp.bfloat16)


def build_toeplitz(kernel_taps, length):
    lag_index = (
        jnp.arange(length, dtype=jnp.int32)[:, None] - jnp.arange(length, dtype=jnp.int32)[None, :]
    )
    toeplitz = jnp.zeros((length, length), jnp.float32)
    for offset in range(kernel_taps.shape[0]):
        toeplitz = toeplitz + jnp.where(
            lag_index == offset, kernel_taps[offset].astype(jnp.float32), jnp.float32(0.0)
        )
    return toeplitz.astype(jnp.bfloat16)


def high_dot(left, right):
    return jnp.dot(left, right, precision=lax.Precision.HIGHEST, preferred_element_type=jnp.float32)


def shards(frames, sketch, kernel_taps):
    filtered = filter_volumes(frames)
    per_device = frames.shape[0]
    flattened = filtered.reshape(per_device, -1)
    voxel_count = flattened.shape[1]
    group_size = lax.axis_size(("wide", "narrow"))
    block = voxel_count // group_size
    length = per_device * group_size
    toeplitz = build_toeplitz(kernel_taps, length)
    arranged = flattened.reshape(1, per_device, group_size, block)
    received = lax.all_to_all(arranged, ("wide", "narrow"), split_axis=2, concat_axis=0, tiled=True)
    deconvolved = jnp.dot(
        toeplitz, received.reshape(length, received.shape[3]), preferred_element_type=jnp.float32
    ).astype(jnp.bfloat16)
    sketched = lax.dot_general(
        sketch, deconvolved, (((0,), (0,)), ((), ())), preferred_element_type=jnp.float32
    )
    deconvolved, sketched = (deconvolved, sketched)
    series = deconvolved.astype(jnp.float32)
    local_gram = (
        lax.dot_general(
            deconvolved, deconvolved, (((1,), (1,)), ((), ())), preferred_element_type=jnp.float32
        )
        / voxel_count
    )
    data_gram = lax.psum(local_gram, ("wide", "narrow"))
    sketch_full = sketch.astype(jnp.float32)
    weighted = high_dot(data_gram, sketch_full)
    first_lower = jnp.linalg.cholesky(high_dot(sketch_full.T, weighted))
    projected = jax.scipy.linalg.solve_triangular(first_lower, weighted.T, lower=True).T
    second_lower = jnp.linalg.cholesky(high_dot(projected.T, high_dot(data_gram, projected)))
    combined = jax.scipy.linalg.solve_triangular(second_lower, projected.T, lower=True)
    basis = high_dot(combined, series)
    factor = second_lower.T
    return (basis, factor)


def solution(mesh):
    return jax.shard_map(
        shards,
        mesh=mesh,
        in_specs=(P(("wide", "narrow"), None, None, None), P(), P()),
        out_specs=(P(None, ("wide", "narrow")), P()),
        check_vma=False,
    )
```

profile of v0, /device:TPU:0, one launch (start us, length us, event | category | flops | bytes accessed | tf_op | source)
XLA Modules:
  0.0 296.3 jit_solution(4108505157623894362)
XLA Ops:
  9.1 0.7 fusion.341
  10.4 0.7 fusion.342
  11.1 9.6 %select_add_fusion.1 = f32[128,256]{1,0:T(8,128)S(1)} fusion(f32[]{:T(128)} %bitcast.78, f32[]{:T(128)} %bitcast.77, f32[]{:T(128)} %bitcast.76, f32[]{:T(128)} %bitcast.75, f32[]{:T(128)} %bitcast.74, f32[]{:T(128)} %bitcast.73, f32[]{:T(128)} %bitcast.72, f32[]{:T(128)} %bitcast.71, f32[]{:T(128)} %bitcast.70, f32[]{:T(128)} %bitcast.69, f32[]{:T(128)} %bitcast.68, ...), kind=kLoop, calls=%fused_computation.85 | loop fusion | flops 1507328 | bytes 131644 | tf_op jit(solution)/shard_map/add | solution.py:23
  20.7 9.7 %select_add_fusion = f32[128,256]{1,0:T(8,128)S(1)} fusion(f32[]{:T(128)} %bitcast.93, f32[]{:T(128)} %bitcast.92, f32[]{:T(128)} %bitcast.91, f32[]{:T(128)} %bitcast.90, f32[]{:T(128)} %bitcast.89, f32[]{:T(128)} %bitcast.88, f32[]{:T(128)} %bitcast.87, f32[]{:T(128)} %bitcast.86, f32[]{:T(128)} %bitcast.85, f32[]{:T(128)} %bitcast.84, f32[]{:T(128)} %bitcast.83, ...), kind=kLoop, calls=%fused_computation.84 | loop fusion | flops 1507328 | bytes 131644 | tf_op jit(solution)/shard_map/add | solution.py:23
  30.4 1.9 convolution_bitcast_fusion
  32.3 11.5 %fusion = f32[8,2,128,128]{3,2,1,0:T(8,128)S(1)} fusion(f32[8,2,256,256]{2,3,1,0:T(8,128)S(1)} %convolution_bitcast_fusion, f32[]{:T(128)} %bitcast.93, f32[]{:T(128)} %bitcast.92, f32[]{:T(128)} %bitcast.91, f32[]{:T(128)} %bitcast.90, f32[]{:T(128)} %bitcast.89, f32[]{:T(128)} %bitcast.88, f32[]{:T(128)} %bitcast.87, f32[]{:T(128)} %bitcast.86, ...), kind=kOutput, calls=%fused_computation.1 | convolution fusion | flops 806813696 | bytes 3146300 | tf_op jit(solution)/shard_map/or,...rc->...oc/dot_general | solution.py:44
  43.8 11.4 %fusion.10 = bf16[8,2,128,128]{2,3,1,0:T(8,128)(2,1)S(1)} fusion(f32[8,2,128,128]{3,2,1,0:T(8,128)S(1)} %fusion, f32[8,2,256,256]{2,3,1,0:T(8,128)S(1)} %convolution_bitcast_fusion, f32[]{:T(128)} %bitcast.78, f32[]{:T(128)} %bitcast.77, f32[]{:T(128)} %bitcast.76, f32[]{:T(128)} %bitcast.75, f32[]{:T(128)} %bitcast.74, f32[]{:T(128)} %bitcast.73, ...), kind=kOutput, calls=%fused_computation.8 | convolution fusion | flops 807337984 | bytes 3670588 | tf_op jit(solution)/shard_map/or,...rc->...oc/dot_general | solution.py:38
  55.7 1.1 copy.14
  56.8 7.3 %all-to-all-start = ((bf16[1,8,32,1024]{3,1,0,2:T(8,128)(2,1)}), bf16[1,8,32,1024]{3,1,0,2:T(8,128)(2,1)S(1)}, u32[]{:S(2)}, u32[]{:S(2)}) async-start(bf16[1,8,32,1024]{3,1,0,2:T(8,128)(2,1)} %copy.14), calls=%async_computation | async-start | bytes 1048576 | tf_op jit(solution)/shard_map/all_to_all | solution.py:79
  64.4 0.7 fusion.338
  70.2 0.7 fusion.337
  83.5 0.7 fusion.339
  102.4 0.7 fusion.340
  107.5 1.1 convolution_convert_fusion
  108.6 1.0 convolution_multiply_fusion
  109.7 128.0 %all-reduce.2.cloned.1.call-done = f32[256,256]{1,0:T(8,128)} async-done(((f32[256,256]{1,0:T(8,128)}), f32[256,256]{1,0:T(8,128)}) %all-reduce.2.cloned.1.call-update) | async-done | bytes 262160 | tf_op jit(solution)/shard_map/psum | solution.py:94
  237.7 1.2 fusion.343
  239.3 11.7 %cholesky.44 = f32[128,128]{1,0:T(8,128)S(1)} custom-call(f32[128,128]{1,0:T(8,128)S(1)} %add_multiply_fusion), custom_call_target="Cholesky" | custom-call | tf_op jit(solution)/shard_map/jit(cholesky)/cholesky | solution.py:97
  252.4 9.8 %custom-call.6 = f32[1,128,128]{1,2,0:T(8,128)S(1)} custom-call(f32[1,128,128]{2,1,0:T(8,128)S(1)} %fusion.228), custom_call_target="InvertDiagBlocksLowerTriangular" | custom-call | tf_op jit(solution)/shard_map/jit(_solve_triangular)/triangular_solve | solution.py:98
  262.5 1.3 fusion.345
  264.2 11.9 %cholesky.55 = f32[128,128]{1,0:T(8,128)S(1)} custom-call(f32[128,128]{1,0:T(8,128)S(1)} %fusion.231), custom_call_target="Cholesky" | custom-call | tf_op jit(solution)/shard_map/jit(cholesky)/cholesky | solution.py:99
  277.4 9.8 %custom-call.7 = f32[1,128,128]{1,2,0:T(8,128)S(1)} custom-call(f32[1,128,128]{2,1,0:T(8,128)S(1)} %get-tuple-element.11), custom_call_target="InvertDiagBlocksLowerTriangular" | custom-call | tf_op jit(solution)/shard_map/jit(_solve_triangular)/triangular_solve | solution.py:100
  287.6 1.2 fusion.347
  288.7 0.7 copy.17
  (30 shorter events, 7.4 us)
Async XLA Ops:
  7.2 23.2 %copy-start = (bf16[8,2,256,256]{3,2,1,0:T(8,128)(2,1)S(1)}, bf16[8,2,256,256]{3,2,1,0:T(8,128)(2,1)}, u32[]{:S(2)}) copy-start(bf16[8,2,256,256]{3,2,1,0:T(8,128)(2,1)} %param.6) | copy-start | bytes 6291460
  55.2 9.2 %copy-start.1 = (bf16[64]{0:T(256)(128)(2,1)S(1)}, bf16[64]{0:T(256)(128)(2,1)}, u32[]{:S(2)}) copy-start(bf16[64]{0:T(256)(128)(2,1)} %param.8) | copy-start | bytes 388
  56.8 50.7 %all-to-all-start = ((bf16[1,8,32,1024]{3,1,0,2:T(8,128)(2,1)}), bf16[1,8,32,1024]{3,1,0,2:T(8,128)(2,1)S(1)}, u32[]{:S(2)}, u32[]{:S(2)}) async-start(bf16[1,8,32,1024]{3,1,0,2:T(8,128)(2,1)} %copy.14), calls=%async_computation | async-start | bytes 1048576 | tf_op jit(solution)/shard_map/all_to_all | solution.py:79
  64.2 173.5 %all-reduce.2.cloned.1.call-start = ((), (), s32[]{:S(2)}) async-start(), calls=%async_computation.1 | async-start | bytes 524288 | tf_op jit(solution)/shard_map/psum | solution.py:94
  107.5 130.2 %copy-start.2 = (bf16[256,128]{1,0:T(8,128)(2,1)S(1)}, bf16[256,128]{1,0:T(8,128)(2,1)}, u32[]{:S(2)}) copy-start(bf16[256,128]{1,0:T(8,128)(2,1)} %param.7) | copy-start | bytes 196612
Sparse Core Ops, SparseCore 0:
  109.8 127.8 all-reduce.1
where the time goes:
time: 298 us; the launch traced here: 296 us
  waiting for transfers between devices  128 us (43%)
  other arithmetic  67.7 us (23%)
  between operations  54.4 us (18%)
  matrix products  31.8 us (11%)
  starting transfers between devices  7.54 us (3%)
  local copies, waits for them, and re-layouts  6.83 us (2%)
    psum x1, waiting for transfers between devices, shards(): data_gram = lax.psum(local_gram, ('wide', 'narrow'))  128 us
    add x2, other arithmetic, band_matrix(): matrix + jnp.where(offset_index == offset, weights[offset], jnp.float32(0...  19.2 us
    another operation x3, other arithmetic, shards(): jnp.linalg.cholesky(high_dot(projected.T, high_dot(data_gram, projected)))  12.6 us
    another operation x3, other arithmetic, shards(): first_lower = jnp.linalg.cholesky(high_dot(sketch_full.T, weighted))  12.4 us
    dot_general x1, matrix products, filter_volumes(): jnp.einsum('or,...rc->...oc', band_matrix(3.0, row_count), column_pass[.....  11.5 us
    dot_general x1, matrix products, filter_volumes(): jnp.einsum('or,...rc->...oc', band_matrix(1.5, row_count), column_pass[.....  11.4 us
    another operation x2, other arithmetic, shards(): jax.scipy.linalg.solve_triangular(first_lower, weighted.T, lower=True)  10.5 us
    another operation x1, other arithmetic, shards(): jax.scipy.linalg.solve_triangular(second_lower, projected.T, lower=True)  9.81 us
  transfers between devices with their start and end apart: 2, of which 1 were waited for; matrix products, arithmetic and copies ran while one was open for 1% of the time, Pallas kernels for 0%

commit v1 on v0

v1 whole, which is shorter than its diff:
```python
import functools

import jax
import jax.numpy as jnp
import numpy as np
from jax import lax
from jax.experimental import pallas as pl
from jax.experimental.pallas import tpu as pltpu
from jax.sharding import PartitionSpec as P

AXES = ("wide", "narrow")
SUB = 8
LANES = 128


def gauss_taps(spread):
    position = np.arange(15, dtype=np.float32) - np.float32(7.0)
    weights = np.exp(-position * position / np.float32(2.0 * spread * spread))
    return (weights / np.sum(weights, dtype=np.float32)).astype(np.float32)


def band_matrix(spread, length):
    outputs = length // 2
    offset = np.arange(length)[None, :] - 2 * np.arange(outputs)[:, None] + 7
    weights = gauss_taps(spread)
    inside = (offset >= 0) & (offset < 15)
    return np.where(inside, weights[np.clip(offset, 0, 14)], np.float32(0.0))


def split_constant(matrix):
    high = matrix.astype(jnp.bfloat16)
    low = (matrix - high.astype(np.float32)).astype(jnp.bfloat16)
    return high, low


def dot(left, right, contract=((1,), (0,))):
    return lax.dot_general(left, right, (contract, ((), ())), preferred_element_type=jnp.float32)


def exact_dot(left, right, contract=((1,), (0,))):
    return lax.dot_general(
        left,
        right,
        (contract, ((), ())),
        precision=lax.Precision.HIGHEST,
        preferred_element_type=jnp.float32,
    )


def split(value, parts):
    pieces = []
    for _ in range(parts):
        piece = value.astype(jnp.bfloat16)
        pieces.append(piece)
        value = value - piece.astype(jnp.float32)
    return pieces


def filter_kernel(frames, row_bands, col_bands, out, held, planes, sems):
    count, plane_count = frames.shape[0], frames.shape[1]
    half_rows, half_cols = row_bands.shape[0] // 4, col_bands.shape[1] // 2
    copies = []
    for t in range(count):
        copy = pltpu.make_async_copy(frames.at[t], held.at[t], sems.at[t])
        copy.start()
        copies.append(copy)
    for t in range(count):
        copies[t].wait()
        narrow, broad = [], []
        for p in range(plane_count):
            passed = dot(row_bands[...], held[t, p])
            both = passed[: 2 * half_rows] + passed[2 * half_rows :]
            narrow.append(both[:half_rows])
            broad.append(both[half_rows:])
        narrow = jnp.concatenate(narrow, axis=0)
        broad = jnp.concatenate(broad, axis=0)
        length = narrow.shape[1]
        parts = zip(split(narrow, 2), split(broad, 2))
        (narrow_high, broad_high), (narrow_low, broad_low) = parts
        wide_sum = dot(narrow_high, col_bands[:length]) + dot(broad_high, col_bands[length:])
        low_sum = dot(narrow_low, col_bands[:length, :half_cols]) + dot(
            broad_low, col_bands[length:, :half_cols]
        )
        planes[:, t, :] = wide_sum[:, :half_cols] + (wide_sum[:, half_cols:] + low_sum)
    out[...] = planes[...].astype(jnp.bfloat16).reshape(out.shape)


def filter_call(frames, groups):
    count, plane_count, rows, cols = frames.shape
    narrow_high, narrow_low = split_constant(band_matrix(1.5, rows))
    broad_high, broad_low = split_constant(band_matrix(3.0, rows))
    row_bands = np.concatenate([narrow_high, broad_high, narrow_low, broad_low], axis=0)
    narrow_high, narrow_low = split_constant(band_matrix(1.5, cols).T)
    broad_high, broad_low = split_constant(-band_matrix(3.0, cols).T)
    col_bands = np.concatenate(
        [
            np.concatenate([narrow_high, narrow_low], axis=1),
            np.concatenate([broad_high, broad_low], axis=1),
        ],
        axis=0,
    )
    lines = plane_count * (rows // 2)
    shape = (groups, lines // groups, count, cols // 2)
    vmem = pl.BlockSpec(memory_space=pltpu.VMEM)
    return pl.pallas_call(
        filter_kernel,
        out_shape=jax.ShapeDtypeStruct(shape, jnp.bfloat16),
        in_specs=[pl.BlockSpec(memory_space=pl.ANY), vmem, vmem],
        out_specs=vmem,
        scratch_shapes=[
            pltpu.VMEM(frames.shape, jnp.bfloat16),
            pltpu.VMEM((lines, count, cols // 2), jnp.float32),
            pltpu.SemaphoreType.DMA((count,)),
        ],
        name="filter_volumes",
    )(frames, jnp.asarray(row_bands), jnp.asarray(col_bands))


def deconvolve_kernel(voxel_count, taps, received, deconvolved, gram):
    length = deconvolved.shape[0]
    taps_row = jnp.concatenate(
        [taps[...].astype(jnp.float32), jnp.zeros((1, length - taps.shape[1]), jnp.float32)], axis=1
    )
    lags = pltpu.roll(
        jnp.broadcast_to(taps_row, (length, length)), 0, 1, stride=1, stride_axis=0
    )
    source = lax.broadcasted_iota(jnp.int32, (length, length), 0)
    target = lax.broadcasted_iota(jnp.int32, (length, length), 1)
    toeplitz = jnp.where(target >= source, lags, 0.0).T.astype(jnp.bfloat16)
    if len(received.shape) == 4:
        lines = [
            received[:, r].astype(jnp.float32).reshape(length, received.shape[3]).astype(jnp.bfloat16)
            for r in range(received.shape[1])
        ]
    else:
        lines = [received[r] for r in range(received.shape[0])]
    series = dot(toeplitz, jnp.concatenate(lines, axis=1)).astype(jnp.bfloat16)
    deconvolved[...] = series
    full = dot(series, series, ((1,), (1,))) * (1.0 / voxel_count)
    half = length // 2
    gram[:half] = full[:half, :half]
    gram[half:length] = full[half:, :half]
    gram[length:] = full[half:, half:]


def deconvolve_call(kernel_taps, received, voxel_count):
    groups, lines, count, width = received.shape
    length = groups * count
    if count % SUB:
        received = jnp.swapaxes(received, 0, 1).reshape(lines, length, width)
    vmem = pl.BlockSpec(memory_space=pltpu.VMEM)
    return pl.pallas_call(
        functools.partial(deconvolve_kernel, voxel_count),
        out_shape=(
            jax.ShapeDtypeStruct((length, lines * width), jnp.bfloat16),
            jax.ShapeDtypeStruct((length + length // 2, length // 2), jnp.float32),
        ),
        in_specs=[vmem, vmem],
        out_specs=(vmem, vmem),
        name="deconvolve_gram",
    )(kernel_taps.reshape(1, -1), received)


def exchange(value, mask, size):
    return lax.ppermute(value, AXES, [(i, i ^ mask) for i in range(size)])


def sum_over_devices(packed, size):
    bits = size.bit_length() - 1
    rows = packed.shape[0] // 2
    start = (lax.axis_index(AXES) % 2) * rows
    other = exchange(packed, 1, size)
    half = lax.dynamic_slice_in_dim(packed, start, rows) + lax.dynamic_slice_in_dim(
        other, start, rows
    )
    first = [exchange(half, mask, size) for mask in (2, 4, 6)]
    half = (half + first[0]) + (first[1] + first[2])
    bit = 3
    while bit < bits:
        half = half + exchange(half, 1 << bit, size)
        if bit + 1 < bits:
            half = half + exchange(half, 3 << bit, size)
        bit += 2
    return half, exchange(half, 1, size)


def eliminate(gram):
    size = gram.shape[0]
    blocks = size // SUB
    identity = (
        lax.broadcasted_iota(jnp.int32, (size, size), 0)
        == lax.broadcasted_iota(jnp.int32, (size, size), 1)
    ).astype(jnp.float32)
    left = [gram[SUB * i : SUB * (i + 1)] for i in range(blocks)]
    right = [identity[SUB * i : SUB * (i + 1)] for i in range(blocks)]
    row = lax.broadcasted_iota(jnp.int32, (SUB, size), 0)
    lane = lax.broadcasted_iota(jnp.int32, (SUB, size), 1)

    def columns(block, k):
        return [
            jnp.broadcast_to(block[:, SUB * k + j : SUB * k + j + 1], (SUB, size))
            for j in range(SUB)
        ]

    upper, inverse = [], []
    for k in range(blocks):
        cols = columns(left[k], k)
        steps = []
        pivots = jnp.ones((SUB, size), jnp.float32)
        for j in range(SUB):
            pivot = jnp.broadcast_to(cols[j][j : j + 1], (SUB, size))
            reciprocal = 1.0 / pivot
            pivots = jnp.where(row == j, pivot, pivots)
            tops = [
                jnp.broadcast_to(cols[jj][j : j + 1], (SUB, size)) for jj in range(j + 1, SUB)
            ]
            left_row = jnp.broadcast_to(left[k][j : j + 1], (SUB, size))
            right_row = jnp.broadcast_to(right[k][j : j + 1], (SUB, size))
            ratio = jnp.where(row > j, cols[j] * reciprocal, 0.0)
            for jj in range(j + 1, SUB):
                cols[jj] = cols[jj] - ratio * tops[jj - j - 1]
            left[k] = left[k] - ratio * left_row
            right[k] = right[k] - ratio * right_row
            steps.append((reciprocal, tops, left_row, right_row))
        scale = lax.rsqrt(pivots)
        upper.append(jnp.where(lane >= row + SUB * k, left[k] * scale, 0.0))
        inverse.append(right[k] * scale)
        for i in range(k + 1, blocks):
            cols = columns(left[i], k)
            for j, (reciprocal, tops, left_row, right_row) in enumerate(steps):
                ratio = cols[j] * reciprocal
                for jj in range(j + 1, SUB):
                    cols[jj] = cols[jj] - ratio * tops[jj - j - 1]
                left[i] = left[i] - ratio * left_row
                right[i] = right[i] - ratio * right_row
    return jnp.concatenate(upper, axis=0), jnp.concatenate(inverse, axis=0)


def basis_kernel(lower_half, upper_half, sketch, deconvolved, basis, factor):
    half = lower_half.shape[1]
    rows = lower_half.shape[0]
    packed = jnp.concatenate([lower_half[...], upper_half[...]], axis=0)
    corner = packed[half : 2 * half]
    data_gram = jnp.concatenate(
        [
            jnp.concatenate([packed[:half], corner.T], axis=1),
            jnp.concatenate([corner, packed[2 * half :]], axis=1),
        ],
        axis=0,
    )
    weights = sketch[...]
    high, middle, low = split(data_gram, 3)
    weighted = dot(high, weights) + (dot(middle, weights) + dot(low, weights))
    high, middle, low = split(weighted, 3)
    rows_first = ((0,), (0,))
    gram = dot(weights, high, rows_first) + (
        dot(weights, middle, rows_first) + dot(weights, low, rows_first)
    )
    _, inverse = eliminate(gram)
    projected = exact_dot(inverse, weighted, ((1,), (1,)))
    gram = exact_dot(exact_dot(projected, data_gram), projected, ((1,), (1,)))
    upper, inverse = eliminate(gram)
    factor[...] = upper
    high, middle, low = split(exact_dot(inverse, projected), 3)
    series = deconvolved[...]
    basis[...] = dot(high, series) + (dot(middle, series) + dot(low, series))


def basis_call(lower_half, upper_half, sketch, deconvolved):
    rank = sketch.shape[1]
    vmem = pl.BlockSpec(memory_space=pltpu.VMEM)
    return pl.pallas_call(
        basis_kernel,
        out_shape=(
            jax.ShapeDtypeStruct((rank, deconvolved.shape[1]), jnp.float32),
            jax.ShapeDtypeStruct((rank, rank), jnp.float32),
        ),
        in_specs=[vmem] * 4,
        out_specs=(vmem, vmem),
        name="orthonormal_basis",
    )(lower_half, upper_half, sketch, deconvolved)


def shards(size, frames, sketch, kernel_taps):
    voxel_count = frames.shape[1] * (frames.shape[2] // 2) * (frames.shape[3] // 2)
    filtered = filter_call(frames, size)
    received = lax.all_to_all(filtered, AXES, split_axis=0, concat_axis=0, tiled=True)
    deconvolved, packed = deconvolve_call(kernel_taps, received, voxel_count)
    mine, pairs = sum_over_devices(packed, size)
    second = lax.axis_index(AXES) % 2 == 1
    lower_half = jnp.where(second, pairs, mine)
    upper_half = jnp.where(second, mine, pairs)
    return basis_call(lower_half, upper_half, sketch, deconvolved)


def solution(mesh):
    size = mesh.shape["wide"] * mesh.shape["narrow"]
    return jax.shard_map(
        functools.partial(shards, size),
        mesh=mesh,
        in_specs=(P(AXES, None, None, None), P(), P()),
        out_specs=(P(None, AXES), P()),
        check_vma=False,
    )
```

time: 298 us -> 70.1 us (0.24)
  waiting for transfers between devices: 128 us -> 16.7 us
  other arithmetic: 67.7 us -> 1.64 us
  between operations: 54.4 us -> 0.67 us
  matrix products: 31.8 us -> 0 us
  blocking collectives: 0 us -> 23.1 us
  Pallas kernels: 0 us -> 22.2 us
  local copies, waits for them, and re-layouts: 6.83 us -> 0 us
    psum x1 -> x0, waiting for transfers between devices: 128 us -> none  [shards(): data_gram = lax.psum(local_gram, ('wide', 'narrow'))]
    another operation x9 -> x0, other arithmetic: 45.2 us -> none  [the longest x3 12.6 us: shards(): jnp.linalg.cholesky(high_dot(projected.T, high_dot(data_gram, projected)))]
    dot_general x10 -> x0, matrix products: 31.2 us -> none  [the longest x1 11.5 us: filter_volumes(): jnp.einsum('or,...rc->...oc', band_matrix(3.0, row_count), column_pass[.....]
    all_to_all x0 -> x1, blocking collectives: none -> 23.1 us  [shards(): lax.all_to_all(filtered, AXES, split_axis=0, concat_axis=0, tiled=True)]
    pallas_call x0 -> x3, Pallas kernels: none -> 22.2 us  [the longest x1 12.2 us: basis_call(): pl.pallas_call(basis_kernel, out_shape=(jax.ShapeDtypeStruct((rank, decon...]
    add x2 -> x4, other arithmetic: 19.2 us -> 0.95 us  [the longest x1 0.9 us: sum_over_devices(): lax.dynamic_slice_in_dim(packed, start, rows)]
    ppermute x0 -> x7, waiting for transfers between devices: none -> 16.7 us  [exchange(): return lax.ppermute(value, AXES, [(i, i ^ mask) for i in range(size)])]
    all_to_all x1 -> x0, starting transfers between devices: 7.32 us -> none  [shards(): lax.all_to_all(arranged, ('wide', 'narrow'), split_axis=2, concat_axis=0,...]
  transfers between devices with their start and end apart: 2 -> 7, of which waited for: 1 -> 6; matrix products, arithmetic and copies ran while one was open for 1% -> 0% of each run, Pallas kernels for 0% -> 0%
where the time goes in v1:
time: 70.1 us; the launch traced here: 69.8 us
  blocking collectives  23.1 us (33%)
  Pallas kernels  22.2 us (32%)
  waiting for transfers between devices  16.7 us (24%)
  starting transfers between devices  5.55 us (8%)
  other arithmetic  1.64 us (2%)
    all_to_all x1, blocking collectives, shards(): lax.all_to_all(filtered, AXES, split_axis=0, concat_axis=0, tiled=True)  23.1 us
    ppermute x7, waiting for transfers between devices, exchange(): return lax.ppermute(value, AXES, [(i, i ^ mask) for i in range(size)])  16.7 us
    pallas_call x1, Pallas kernels, basis_call(): pl.pallas_call(basis_kernel, out_shape=(jax.ShapeDtypeStruct((rank, decon...  12.2 us
    pallas_call x1, Pallas kernels, filter_call(): pl.pallas_call(filter_kernel, out_shape=jax.ShapeDtypeStruct(shape, jnp.b...  7.53 us
    ppermute x7, starting transfers between devices, exchange(): return lax.ppermute(value, AXES, [(i, i ^ mask) for i in range(size)])  5.55 us
    pallas_call x1, Pallas kernels, deconvolve_call(): pl.pallas_call(functools.partial(deconvolve_kernel, voxel_count), out_sha...  2.47 us
  transfers between devices with their start and end apart: 7, of which 6 were waited for; matrix products, arithmetic and copies ran while one was open for 0% of the time, Pallas kernels for 0%

profile of v1, /device:TPU:0, one launch (start us, length us, event | category | flops | bytes accessed | tf_op | source)
XLA Modules:
  0.0 69.8 jit_solution(15598589715366535820)
XLA Ops:
  0.6 7.5 %filter_volumes.1 = bf16[32,8,8,128]{3,2,1,0:T(8,128)(2,1)} custom-call(bf16[8,2,256,256]{3,2,1,0:T(8,128)(2,1)} %frames.1, bf16[512,256]{1,0:T(8,128)(2,1)} %constant.36.clone.row_bands, bf16[512,256]{1,0:T(8,128)(2,1)} %constant.37.clone.col_bands), custom_call_target="tpu_custom_call" | custom-call | tf_op jit(solution)/shard_map/filter_volumes/pallas_call | solution.py:105
  8.2 23.1 %all_to_all.5.received = bf16[32,8,8,128]{3,2,1,0:T(8,128)(2,1)} all-to-all(bf16[32,8,8,128]{3,2,1,0:T(8,128)(2,1)} %filter_volumes.1), channel_id=1, replica_groups=mesh['wide'=8,'narrow'=4] {'wide','narrow'}, dimensions={0} | all-to-all | bytes 1048576 | tf_op jit(solution)/shard_map/all_to_all | solution.py:287
  31.2 2.5 %deconvolve_gram.1 = (bf16[256,1024]{1,0:T(8,128)(2,1)}, f32[384,128]{1,0:T(8,128)}) custom-call(bf16[1,64]{1,0:T(2,128)(2,1)} %bitcast.1, bf16[32,8,8,128]{3,2,1,0:T(8,128)(2,1)} %all_to_all.5.received), custom_call_target="tpu_custom_call" | custom-call | tf_op jit(solution)/shard_map/deconvolve_gram/pallas_call | solution.py:152
  33.7 0.0 collective-permute-start
  33.7 1.6 %collective-permute-done = f32[384,128]{1,0:T(8,128)S(1)} collective-permute-done((f32[384,128]{1,0:T(8,128)}, f32[384,128]{1,0:T(8,128)S(1)}, u32[]{:S(2)}, u32[]{:S(2)}) %collective-permute-start) | collective-permute-done | bytes 196640 | tf_op jit(solution)/shard_map/ppermute | solution.py:165
  35.4 0.9 %dynamic-slice_add_fusion = f32[192,128]{1,0:T(8,128)S(1)} fusion(f32[384,128]{1,0:T(8,128)S(1)} %collective-permute-done, s32[]{:T(128)S(6)} %select_n.27, f32[384,128]{1,0:T(8,128)} %get-tuple-element.4), kind=kLoop, calls=%fused_computation.1 | loop fusion | flops 24576 | bytes 294916 | tf_op jit(solution)/shard_map/add | solution.py:173
  36.3 1.8 %collective-permute-start.3 = (f32[192,128]{1,0:T(8,128)S(1)}, f32[192,128]{1,0:T(8,128)S(1)}, u32[]{:S(2)}, u32[]{:S(2)}) collective-permute-start(f32[192,128]{1,0:T(8,128)S(1)} %dynamic-slice_add_fusion), channel_id=1, source_target_pairs={{0,6},{1,7},{2,4},{3,5},{4,2},{5,3},{6,0},{7,1},{8,14},{9,15},{10,... | collective-permute-start | bytes 294920 | tf_op jit(solution)/shard_map/ppermute | solution.py:165
  38.1 0.6 collective-permute-start.2
  38.6 1.2 %collective-permute-start.1 = (f32[192,128]{1,0:T(8,128)S(1)}, f32[192,128]{1,0:T(8,128)S(1)}, u32[]{:S(2)}, u32[]{:S(2)}) collective-permute-start(f32[192,128]{1,0:T(8,128)S(1)} %dynamic-slice_add_fusion), channel_id=1, source_target_pairs={{0,2},{1,3},{2,0},{3,1},{4,6},{5,7},{6,4},{7,5},{8,10},{9,11},{10,... | collective-permute-start | bytes 294920 | tf_op jit(solution)/shard_map/ppermute | solution.py:165
  39.8 2.6 %collective-permute-done.3 = f32[192,128]{1,0:T(8,128)S(1)} collective-permute-done((f32[192,128]{1,0:T(8,128)S(1)}, f32[192,128]{1,0:T(8,128)S(1)}, u32[]{:S(2)}, u32[]{:S(2)}) %collective-permute-start.3) | collective-permute-done | bytes 98336 | tf_op jit(solution)/shard_map/ppermute | solution.py:165
  42.4 1.8 %collective-permute-done.2 = f32[192,128]{1,0:T(8,128)S(1)} collective-permute-done((f32[192,128]{1,0:T(8,128)S(1)}, f32[192,128]{1,0:T(8,128)S(1)}, u32[]{:S(2)}, u32[]{:S(2)}) %collective-permute-start.2) | collective-permute-done | bytes 98336 | tf_op jit(solution)/shard_map/ppermute | solution.py:165
  44.2 0.0 collective-permute-done.1
  44.2 0.8 %collective-permute-start.4 = (f32[192,128]{1,0:T(8,128)S(1)}, f32[192,128]{1,0:T(8,128)S(1)}, u32[]{:S(2)}, u32[]{:S(2)}) collective-permute-start(f32[192,128]{1,0:T(8,128)S(1)} %add_add_fusion), channel_id=1, source_target_pairs={{0,8},{1,9},{2,10},{3,11},{4,12},{5,13},{6,14},{7,15},{8,0},{9,1},... | collective-permute-start | bytes 294920 | tf_op jit(solution)/shard_map/ppermute | solution.py:165
  45.0 3.9 %collective-permute-done.4 = f32[192,128]{1,0:T(8,128)S(1)} collective-permute-done((f32[192,128]{1,0:T(8,128)S(1)}, f32[192,128]{1,0:T(8,128)S(1)}, u32[]{:S(2)}, u32[]{:S(2)}) %collective-permute-start.4) | collective-permute-done | bytes 98336 | tf_op jit(solution)/shard_map/ppermute | solution.py:165
  49.0 1.1 %collective-permute-start.5 = (f32[192,128]{1,0:T(8,128)S(1)}, f32[192,128]{1,0:T(8,128)S(1)}, u32[]{:S(2)}, u32[]{:S(2)}) collective-permute-start(f32[192,128]{1,0:T(8,128)S(1)} %add.38), channel_id=1, source_target_pairs={{0,24},{1,25},{2,26},{3,27},{4,28},{5,29},{6,30},{7,31},{8,16},{9,... | collective-permute-start | bytes 294920 | tf_op jit(solution)/shard_map/ppermute | solution.py:165
  50.1 5.5 %collective-permute-done.5 = f32[192,128]{1,0:T(8,128)S(1)} collective-permute-done((f32[192,128]{1,0:T(8,128)S(1)}, f32[192,128]{1,0:T(8,128)S(1)}, u32[]{:S(2)}, u32[]{:S(2)}) %collective-permute-start.5) | collective-permute-done | bytes 98336 | tf_op jit(solution)/shard_map/ppermute | solution.py:165
  55.6 0.1 collective-permute-start.6
  55.7 1.3 %collective-permute-done.6 = f32[192,128]{1,0:T(8,128)S(1)} collective-permute-done((f32[192,128]{1,0:T(8,128)S(1)}, f32[192,128]{1,0:T(8,128)S(1)}, u32[]{:S(2)}, u32[]{:S(2)}) %collective-permute-start.6) | collective-permute-done | bytes 98336 | tf_op jit(solution)/shard_map/ppermute | solution.py:165
  57.0 0.7 broadcast_select_fusion
  57.7 12.2 %orthonormal_basis.1 = (f32[128,1024]{1,0:T(8,128)}, f32[128,128]{1,0:T(8,128)}) custom-call(f32[192,128]{1,0:T(8,128)} %get-tuple-element.7.lower_half, f32[192,128]{1,0:T(8,128)} %get-tuple-element.6.upper_half, bf16[256,128]{1,0:T(8,128)(2,1)} %sketch.1, bf16[256,1024]{1,0:T(8,128)(2,1)} %get-tuple-element.5.deconvolved), custom_call_target="tpu_custom_call" | custom-call | tf_op jit(solution)/shard_map/orthonormal_basis/pallas_call | solution.py:272
  (3 shorter events, 0.0 us)
Async XLA Ops:
  33.7 1.7 %collective-permute-start = (f32[384,128]{1,0:T(8,128)}, f32[384,128]{1,0:T(8,128)S(1)}, u32[]{:S(2)}, u32[]{:S(2)}) collective-permute-start(f32[384,128]{1,0:T(8,128)} %get-tuple-element.4), channel_id=1, source_target_pairs={{0,1},{1,0},{2,3},{3,2},{4,5},{5,4},{6,7},{7,6},{8,9},{9,8},{10,11... | collective-permute-start | bytes 589832 | tf_op jit(solution)/shard_map/ppermute | solution.py:165
  36.3 6.1 %collective-permute-start.3 = (f32[192,128]{1,0:T(8,128)S(1)}, f32[192,128]{1,0:T(8,128)S(1)}, u32[]{:S(2)}, u32[]{:S(2)}) collective-permute-start(f32[192,128]{1,0:T(8,128)S(1)} %dynamic-slice_add_fusion), channel_id=1, source_target_pairs={{0,6},{1,7},{2,4},{3,5},{4,2},{5,3},{6,0},{7,1},{8,14},{9,15},{10,... | collective-permute-start | bytes 294920 | tf_op jit(solution)/shard_map/ppermute | solution.py:165
  38.1 6.1 %collective-permute-start.2 = (f32[192,128]{1,0:T(8,128)S(1)}, f32[192,128]{1,0:T(8,128)S(1)}, u32[]{:S(2)}, u32[]{:S(2)}) collective-permute-start(f32[192,128]{1,0:T(8,128)S(1)} %dynamic-slice_add_fusion), channel_id=1, source_target_pairs={{0,4},{1,5},{2,6},{3,7},{4,0},{5,1},{6,2},{7,3},{8,12},{9,13},{10,... | collective-permute-start | bytes 294920 | tf_op jit(solution)/shard_map/ppermute | solution.py:165
  38.6 5.5 %collective-permute-start.1 = (f32[192,128]{1,0:T(8,128)S(1)}, f32[192,128]{1,0:T(8,128)S(1)}, u32[]{:S(2)}, u32[]{:S(2)}) collective-permute-start(f32[192,128]{1,0:T(8,128)S(1)} %dynamic-slice_add_fusion), channel_id=1, source_target_pairs={{0,2},{1,3},{2,0},{3,1},{4,6},{5,7},{6,4},{7,5},{8,10},{9,11},{10,... | collective-permute-start | bytes 294920 | tf_op jit(solution)/shard_map/ppermute | solution.py:165
  44.2 4.8 %collective-permute-start.4 = (f32[192,128]{1,0:T(8,128)S(1)}, f32[192,128]{1,0:T(8,128)S(1)}, u32[]{:S(2)}, u32[]{:S(2)}) collective-permute-start(f32[192,128]{1,0:T(8,128)S(1)} %add_add_fusion), channel_id=1, source_target_pairs={{0,8},{1,9},{2,10},{3,11},{4,12},{5,13},{6,14},{7,15},{8,0},{9,1},... | collective-permute-start | bytes 294920 | tf_op jit(solution)/shard_map/ppermute | solution.py:165
  49.0 6.6 %collective-permute-start.5 = (f32[192,128]{1,0:T(8,128)S(1)}, f32[192,128]{1,0:T(8,128)S(1)}, u32[]{:S(2)}, u32[]{:S(2)}) collective-permute-start(f32[192,128]{1,0:T(8,128)S(1)} %add.38), channel_id=1, source_target_pairs={{0,24},{1,25},{2,26},{3,27},{4,28},{5,29},{6,30},{7,31},{8,16},{9,... | collective-permute-start | bytes 294920 | tf_op jit(solution)/shard_map/ppermute | solution.py:165
  55.6 1.4 %collective-permute-start.6 = (f32[192,128]{1,0:T(8,128)S(1)}, f32[192,128]{1,0:T(8,128)S(1)}, u32[]{:S(2)}, u32[]{:S(2)}) collective-permute-start(f32[192,128]{1,0:T(8,128)S(1)} %add.39), channel_id=1, source_target_pairs={{0,1},{1,0},{2,3},{3,2},{4,5},{5,4},{6,7},{7,6},{8,9},{9,8},{10,11... | collective-permute-start | bytes 294920 | tf_op jit(solution)/shard_map/ppermute | solution.py:165

commit v2 on v1

--- a/solution.py
+++ b/solution.py
@@ -64,24 +64,31 @@
         copy = pltpu.make_async_copy(frames.at[t], held.at[t], sems.at[t])
         copy.start()
         copies.append(copy)
-    for t in range(count):
+
+    def row_pass(t):
         copies[t].wait()
         narrow, broad = [], []
         for p in range(plane_count):
             passed = dot(row_bands[...], held[t, p])
-            both = passed[: 2 * half_rows] + passed[2 * half_rows :]
-            narrow.append(both[:half_rows])
-            broad.append(both[half_rows:])
-        narrow = jnp.concatenate(narrow, axis=0)
-        broad = jnp.concatenate(broad, axis=0)
-        length = narrow.shape[1]
-        parts = zip(split(narrow, 2), split(broad, 2))
-        (narrow_high, broad_high), (narrow_low, broad_low) = parts
-        wide_sum = dot(narrow_high, col_bands[:length]) + dot(broad_high, col_bands[length:])
-        low_sum = dot(narrow_low, col_bands[:length, :half_cols]) + dot(
-            broad_low, col_bands[length:, :half_cols]
+            passed = passed[: 2 * half_rows] + passed[2 * half_rows :]
+            narrow.append(passed[:half_rows])
+            broad.append(passed[half_rows:])
+        narrow_high, narrow_low = split(jnp.concatenate(narrow, axis=0), 2)
+        broad_high, broad_low = split(jnp.concatenate(broad, axis=0), 2)
+        return (
+            jnp.concatenate([narrow_high, broad_high], axis=1),
+            jnp.concatenate([narrow_low, broad_low], axis=1),
         )
+
+    def column_pass(t, high, low):
+        wide_sum = dot(high, col_bands[...])
+        low_sum = dot(low, col_bands[:, :half_cols])
         planes[:, t, :] = wide_sum[:, :half_cols] + (wide_sum[:, half_cols:] + low_sum)
+
+    waiting = row_pass(0)
+    for t in range(count):
+        current, waiting = waiting, row_pass(t + 1) if t + 1 < count else None
+        column_pass(t, *current)
     out[...] = planes[...].astype(jnp.bfloat16).reshape(out.shape)
 
 
@@ -116,7 +123,7 @@
     )(frames, jnp.asarray(row_bands), jnp.asarray(col_bands))
 
 
-def deconvolve_kernel(voxel_count, taps, received, deconvolved, gram):
+def deconvolve_kernel(voxel_count, second, taps, received, deconvolved, keep, send):
     length = deconvolved.shape[0]
     taps_row = jnp.concatenate(
         [taps[...].astype(jnp.float32), jnp.zeros((1, length - taps.shape[1]), jnp.float32)], axis=1
@@ -138,12 +145,23 @@
     deconvolved[...] = series
     full = dot(series, series, ((1,), (1,))) * (1.0 / voxel_count)
     half = length // 2
-    gram[:half] = full[:half, :half]
-    gram[half:length] = full[half:, :half]
-    gram[length:] = full[half:, half:]
-
-
-def deconvolve_call(kernel_taps, received, voxel_count):
+    row = lax.broadcasted_iota(jnp.int32, (half, half), 0)
+    lane = lax.broadcasted_iota(jnp.int32, (half, half), 1)
+    early, late = full[:half, :half], full[half:, half:]
+    diagonal = jnp.sum(jnp.where(row == lane, early, 0.0), axis=0, keepdims=True)
+    parts = (
+        jnp.concatenate([full[half:, :half], jnp.broadcast_to(diagonal, (SUB, half))], axis=0),
+        jnp.concatenate([jnp.where(row > lane, early, late), jnp.zeros((SUB, half))], axis=0),
+    )
+    for side in range(2):
+
+        @pl.when(second[0] == side)
+        def _():
+            keep[...] = parts[side]
+            send[...] = parts[1 - side]
+
+
+def deconvolve_call(second, kernel_taps, received, voxel_count):
     groups, lines, count, width = received.shape
     length = groups * count
     if count % SUB:
@@ -153,26 +171,22 @@
         functools.partial(deconvolve_kernel, voxel_count),
         out_shape=(
             jax.ShapeDtypeStruct((length, lines * width), jnp.bfloat16),
-            jax.ShapeDtypeStruct((length + length // 2, length // 2), jnp.float32),
+            jax.ShapeDtypeStruct((length // 2 + SUB, length // 2), jnp.float32),
+            jax.ShapeDtypeStruct((length // 2 + SUB, length // 2), jnp.float32),
         ),
-        in_specs=[vmem, vmem],
-        out_specs=(vmem, vmem),
+        in_specs=[pl.BlockSpec(memory_space=pltpu.SMEM), vmem, vmem],
+        out_specs=(vmem, vmem, vmem),
         name="deconvolve_gram",
-    )(kernel_taps.reshape(1, -1), received)
+    )(second, kernel_taps.reshape(1, -1), received)
 
 
 def exchange(value, mask, size):
     return lax.ppermute(value, AXES, [(i, i ^ mask) for i in range(size)])
 
 
-def sum_over_devices(packed, size):
+def sum_over_devices(keep, send, size):
     bits = size.bit_length() - 1
-    rows = packed.shape[0] // 2
-    start = (lax.axis_index(AXES) % 2) * rows
-    other = exchange(packed, 1, size)
-    half = lax.dynamic_slice_in_dim(packed, start, rows) + lax.dynamic_slice_in_dim(
-        other, start, rows
-    )
+    half = keep + exchange(send, 1, size)
     first = [exchange(half, mask, size) for mask in (2, 4, 6)]
     half = (half + first[0]) + (first[1] + first[2])
     bit = 3
@@ -236,15 +250,21 @@
     return jnp.concatenate(upper, axis=0), jnp.concatenate(inverse, axis=0)
 
 
-def basis_kernel(lower_half, upper_half, sketch, deconvolved, basis, factor):
-    half = lower_half.shape[1]
-    rows = lower_half.shape[0]
-    packed = jnp.concatenate([lower_half[...], upper_half[...]], axis=0)
-    corner = packed[half : 2 * half]
+def basis_kernel(second, mine, pairs, sketch, deconvolved, basis, factor):
+    half = mine.shape[1]
+    is_second = second[0] == 1
+    cross = jnp.where(is_second, pairs[...], mine[...])
+    square = jnp.where(is_second, mine[:half], pairs[:half])
+    corner, diagonal = cross[:half], cross[half : half + 1]
+    row = lax.broadcasted_iota(jnp.int32, (half, half), 0)
+    lane = lax.broadcasted_iota(jnp.int32, (half, half), 1)
+    turned = square.T
+    early = jnp.where(row > lane, square, jnp.where(row < lane, turned, diagonal))
+    late = jnp.where(row > lane, turned, square)
     data_gram = jnp.concatenate(
         [
-            jnp.concatenate([packed[:half], corner.T], axis=1),
-            jnp.concatenate([corner, packed[2 * half :]], axis=1),
+            jnp.concatenate([early, corner.T], axis=1),
+            jnp.concatenate([corner, late], axis=1),
         ],
         axis=0,
     )
@@ -266,7 +286,7 @@
     basis[...] = dot(high, series) + (dot(middle, series) + dot(low, series))
 
 
-def basis_call(lower_half, upper_half, sketch, deconvolved):
+def basis_call(second, mine, pairs, sketch, deconvolved):
     rank = sketch.shape[1]
     vmem = pl.BlockSpec(memory_space=pltpu.VMEM)
     return pl.pallas_call(
@@ -275,22 +295,20 @@
             jax.ShapeDtypeStruct((rank, deconvolved.shape[1]), jnp.float32),
             jax.ShapeDtypeStruct((rank, rank), jnp.float32),
         ),
-        in_specs=[vmem] * 4,
+        in_specs=[pl.BlockSpec(memory_space=pltpu.SMEM)] + [vmem] * 4,
         out_specs=(vmem, vmem),
         name="orthonormal_basis",
-    )(lower_half, upper_half, sketch, deconvolved)
+    )(second, mine, pairs, sketch, deconvolved)
 
 
 def shards(size, frames, sketch, kernel_taps):
     voxel_count = frames.shape[1] * (frames.shape[2] // 2) * (frames.shape[3] // 2)
     filtered = filter_call(frames, size)
     received = lax.all_to_all(filtered, AXES, split_axis=0, concat_axis=0, tiled=True)
-    deconvolved, packed = deconvolve_call(kernel_taps, received, voxel_count)
-    mine, pairs = sum_over_devices(packed, size)
-    second = lax.axis_index(AXES) % 2 == 1
-    lower_half = jnp.where(second, pairs, mine)
-    upper_half = jnp.where(second, mine, pairs)
-    return basis_call(lower_half, upper_half, sketch, deconvolved)
+    second = (lax.axis_index(AXES) % 2).astype(jnp.int32).reshape(1)
+    deconvolved, keep, send = deconvolve_call(second, kernel_taps, received, voxel_count)
+    mine, pairs = sum_over_devices(keep, send, size)
+    return basis_call(second, mine, pairs, sketch, deconvolved)
 
 
 def solution(mesh):

time: 70.1 us -> 68 us (0.970)
  blocking collectives: 23.1 us -> 0 us
  waiting for transfers between devices: 16.7 us -> 29.7 us
  starting transfers between devices: 5.55 us -> 13.3 us
  local copies, waits for them, and re-layouts: 0 us -> 1.43 us
  other arithmetic: 1.64 us -> 0.93 us
    all_to_all x1 -> x0, blocking collectives: 23.1 us -> none  [shards(): lax.all_to_all(filtered, AXES, split_axis=0, concat_axis=0, tiled=True)]
    all_to_all x0 -> x1, waiting for transfers between devices: none -> 15.6 us  [shards(): lax.all_to_all(filtered, AXES, split_axis=0, concat_axis=0, tiled=True)]
    all_to_all x0 -> x1, starting transfers between devices: none -> 7.34 us  [shards(): lax.all_to_all(filtered, AXES, split_axis=0, concat_axis=0, tiled=True)]
    ppermute x7, waiting for transfers between devices: 16.7 us -> 14.1 us  [exchange(): return lax.ppermute(value, AXES, [(i, i ^ mask) for i in range(size)])]
    unnamed x0 -> x6, local copies, waits for them, and re-layouts: none -> 1.43 us
    pallas_call x1, Pallas kernels: 7.53 us -> 6.62 us  [filter_call(): pl.pallas_call(filter_kernel, out_shape=jax.ShapeDtypeStruct(shape, jnp.b...]
  transfers between devices with their start and end apart: 7 -> 8, of which waited for: 6 -> 7; matrix products, arithmetic and copies ran while one was open for 0% -> 0% of each run, Pallas kernels for 0% -> 0%
where the time goes in v2:
time: 68 us; the launch traced here: 67.6 us
  waiting for transfers between devices  29.7 us (44%)
  Pallas kernels  21.6 us (32%)
  starting transfers between devices  13.3 us (20%)
  local copies, waits for them, and re-layouts  1.43 us (2%)
  other arithmetic  0.93 us (1%)
  between operations  0.69 us (1%)
    all_to_all x1, waiting for transfers between devices, shards(): lax.all_to_all(filtered, AXES, split_axis=0, concat_axis=0, tiled=True)  15.6 us
    ppermute x7, waiting for transfers between devices, exchange(): return lax.ppermute(value, AXES, [(i, i ^ mask) for i in range(size)])  14.1 us
    pallas_call x1, Pallas kernels, basis_call(): pl.pallas_call(basis_kernel, out_shape=(jax.ShapeDtypeStruct((rank, decon...  12.1 us
    all_to_all x1, starting transfers between devices, shards(): lax.all_to_all(filtered, AXES, split_axis=0, concat_axis=0, tiled=True)  7.34 us
    pallas_call x1, Pallas kernels, filter_call(): pl.pallas_call(filter_kernel, out_shape=jax.ShapeDtypeStruct(shape, jnp.b...  6.62 us
    ppermute x7, starting transfers between devices, exchange(): return lax.ppermute(value, AXES, [(i, i ^ mask) for i in range(size)])  5.92 us
    pallas_call x1, Pallas kernels, deconvolve_call(): pl.pallas_call(functools.partial(deconvolve_kernel, voxel_count), out_sha...  2.84 us
    unnamed x6, local copies, waits for them, and re-layouts  1.43 us
  transfers between devices with their start and end apart: 8, of which 7 were waited for; matrix products, arithmetic and copies ran while one was open for 0% of the time, Pallas kernels for 0%

profile of v2, /device:TPU:0, one launch (start us, length us, event | category | flops | bytes accessed | tf_op | source)
XLA Modules:
  0.0 67.6 jit_solution(14884000469877820933)
XLA Ops:
  0.6 6.6 %filter_volumes.1 = bf16[32,8,8,128]{3,2,1,0:T(8,128)(2,1)} custom-call(bf16[8,2,256,256]{3,2,1,0:T(8,128)(2,1)} %frames.1, bf16[512,256]{1,0:T(8,128)(2,1)} %constant.28.clone.row_bands, bf16[512,256]{1,0:T(8,128)(2,1)} %constant.29.clone.col_bands), custom_call_target="tpu_custom_call" | custom-call | tf_op jit(solution)/shard_map/filter_volumes/pallas_call | solution.py:112
  7.3 7.3 %all-to-all-start = ((bf16[32,8,8,128]{3,2,1,0:T(8,128)(2,1)}), bf16[32,8,8,128]{3,2,1,0:T(8,128)(2,1)S(1)}, u32[]{:S(2)}, u32[]{:S(2)}) async-start(bf16[32,8,8,128]{3,2,1,0:T(8,128)(2,1)} %filter_volumes.1), calls=%async_computation | async-start | bytes 1048576 | tf_op jit(solution)/shard_map/all_to_all | solution.py:307
  14.6 15.6 %all-to-all-done.received = bf16[32,8,8,128]{3,2,1,0:T(8,128)(2,1)S(1)} async-done(((bf16[32,8,8,128]{3,2,1,0:T(8,128)(2,1)}), bf16[32,8,8,128]{3,2,1,0:T(8,128)(2,1)S(1)}, u32[]{:S(2)}, u32[]{:S(2)}) %all-to-all-start) | async-done | bytes 524320 | tf_op jit(solution)/shard_map/all_to_all | solution.py:307
  30.2 0.8 %copy-done = bf16[32,8,8,128]{3,2,1,0:T(8,128)(2,1)} copy-done((bf16[32,8,8,128]{3,2,1,0:T(8,128)(2,1)}, bf16[32,8,8,128]{3,2,1,0:T(8,128)(2,1)S(1)}, u32[]{:S(2)}) %copy-start) | copy-done | bytes 524312
  31.0 2.8 %deconvolve_gram.1 = (bf16[256,1024]{1,0:T(8,128)(2,1)}, f32[136,128]{1,0:T(8,128)}, f32[136,128]{1,0:T(8,128)}) custom-call(s32[1]{0:T(128)} %bitcast.second, bf16[1,64]{1,0:T(2,128)(2,1)} %bitcast.2, bf16[32,8,8,128]{3,2,1,0:T(8,128)(2,1)} %copy-done), custom_call_target="tpu_custom_call" | custom-call | tf_op jit(solution)/shard_map/deconvolve_gram/pallas_call | solution.py:170
  33.9 0.0 collective-permute-start
  33.9 1.5 %collective-permute-done = f32[136,128]{1,0:T(8,128)S(1)} collective-permute-done((f32[136,128]{1,0:T(8,128)}, f32[136,128]{1,0:T(8,128)S(1)}, u32[]{:S(2)}, u32[]{:S(2)}) %collective-permute-start) | collective-permute-done | bytes 69664 | tf_op jit(solution)/shard_map/ppermute | solution.py:184
  35.3 0.9 %add.27 = f32[136,128]{1,0:T(8,128)S(1)} add(f32[136,128]{1,0:T(8,128)} %get-tuple-element.5, f32[136,128]{1,0:T(8,128)S(1)} %collective-permute-done) | non-fusion elementwise | flops 17408 | bytes 208896 | tf_op jit(solution)/shard_map/add | solution.py:189
  36.2 1.8 %collective-permute-start.3 = (f32[136,128]{1,0:T(8,128)S(1)}, f32[136,128]{1,0:T(8,128)S(1)}, u32[]{:S(2)}, u32[]{:S(2)}) collective-permute-start(f32[136,128]{1,0:T(8,128)S(1)} %add.27), channel_id=1, source_target_pairs={{0,6},{1,7},{2,4},{3,5},{4,2},{5,3},{6,0},{7,1},{8,14},{9,15},{10,... | collective-permute-start | bytes 208904 | tf_op jit(solution)/shard_map/ppermute | solution.py:184
  38.0 0.6 collective-permute-start.2
  38.6 1.2 %collective-permute-start.1 = (f32[136,128]{1,0:T(8,128)S(1)}, f32[136,128]{1,0:T(8,128)S(1)}, u32[]{:S(2)}, u32[]{:S(2)}) collective-permute-start(f32[136,128]{1,0:T(8,128)S(1)} %add.27), channel_id=1, source_target_pairs={{0,2},{1,3},{2,0},{3,1},{4,6},{5,7},{6,4},{7,5},{8,10},{9,11},{10,... | collective-permute-start | bytes 208904 | tf_op jit(solution)/shard_map/ppermute | solution.py:184
  39.8 1.8 %collective-permute-done.3 = f32[136,128]{1,0:T(8,128)S(1)} collective-permute-done((f32[136,128]{1,0:T(8,128)S(1)}, f32[136,128]{1,0:T(8,128)S(1)}, u32[]{:S(2)}, u32[]{:S(2)}) %collective-permute-start.3) | collective-permute-done | bytes 69664 | tf_op jit(solution)/shard_map/ppermute | solution.py:184
  41.5 1.4 %collective-permute-done.2 = f32[136,128]{1,0:T(8,128)S(1)} collective-permute-done((f32[136,128]{1,0:T(8,128)S(1)}, f32[136,128]{1,0:T(8,128)S(1)}, u32[]{:S(2)}, u32[]{:S(2)}) %collective-permute-start.2) | collective-permute-done | bytes 69664 | tf_op jit(solution)/shard_map/ppermute | solution.py:184
  42.9 0.0 collective-permute-done.1
  43.0 0.8 %collective-permute-start.4 = (f32[136,128]{1,0:T(8,128)S(1)}, f32[136,128]{1,0:T(8,128)S(1)}, u32[]{:S(2)}, u32[]{:S(2)}) collective-permute-start(f32[136,128]{1,0:T(8,128)S(1)} %add_add_fusion), channel_id=1, source_target_pairs={{0,8},{1,9},{2,10},{3,11},{4,12},{5,13},{6,14},{7,15},{8,0},{9,1},... | collective-permute-start | bytes 208904 | tf_op jit(solution)/shard_map/ppermute | solution.py:184
  43.8 3.5 %collective-permute-done.4 = f32[136,128]{1,0:T(8,128)S(1)} collective-permute-done((f32[136,128]{1,0:T(8,128)S(1)}, f32[136,128]{1,0:T(8,128)S(1)}, u32[]{:S(2)}, u32[]{:S(2)}) %collective-permute-start.4) | collective-permute-done | bytes 69664 | tf_op jit(solution)/shard_map/ppermute | solution.py:184
  47.3 1.5 %collective-permute-start.5 = (f32[136,128]{1,0:T(8,128)S(1)}, f32[136,128]{1,0:T(8,128)S(1)}, u32[]{:S(2)}, u32[]{:S(2)}) collective-permute-start(f32[136,128]{1,0:T(8,128)S(1)} %add.31), channel_id=1, source_target_pairs={{0,24},{1,25},{2,26},{3,27},{4,28},{5,29},{6,30},{7,31},{8,16},{9,... | collective-permute-start | bytes 208904 | tf_op jit(solution)/shard_map/ppermute | solution.py:184
  48.8 4.7 %collective-permute-done.5 = f32[136,128]{1,0:T(8,128)S(1)} collective-permute-done((f32[136,128]{1,0:T(8,128)S(1)}, f32[136,128]{1,0:T(8,128)S(1)}, u32[]{:S(2)}, u32[]{:S(2)}) %collective-permute-start.5) | collective-permute-done | bytes 69664 | tf_op jit(solution)/shard_map/ppermute | solution.py:184
  53.5 0.0 copy-start.1
  53.5 0.1 collective-permute-start.6
  53.6 1.2 %collective-permute-done.6.pairs = f32[136,128]{1,0:T(8,128)S(1)} collective-permute-done((f32[136,128]{1,0:T(8,128)S(1)}, f32[136,128]{1,0:T(8,128)S(1)}, u32[]{:S(2)}, u32[]{:S(2)}) %collective-permute-start.6) | collective-permute-done | bytes 69664 | tf_op jit(solution)/shard_map/ppermute | solution.py:184
  54.9 0.0 copy-done.1
  54.9 0.6 copy-done.2
  55.5 12.1 %orthonormal_basis.1 = (f32[128,1024]{1,0:T(8,128)}, f32[128,128]{1,0:T(8,128)}) custom-call(s32[1]{0:T(128)} %bitcast.second, f32[136,128]{1,0:T(8,128)} %copy-done.1, f32[136,128]{1,0:T(8,128)} %copy-done.2, bf16[256,128]{1,0:T(8,128)(2,1)} %sketch.1, bf16[256,1024]{1,0:T(8,128)(2,1)} %get-tuple-element.7.deconvolved), custom_call_target="tpu_custom_call" | custom-call | tf_op jit(solution)/shard_map/orthonormal_basis/pallas_call | solution.py:292
  (5 shorter events, 0.0 us)
Async XLA Ops:
  7.3 23.0 %all-to-all-start = ((bf16[32,8,8,128]{3,2,1,0:T(8,128)(2,1)}), bf16[32,8,8,128]{3,2,1,0:T(8,128)(2,1)S(1)}, u32[]{:S(2)}, u32[]{:S(2)}) async-start(bf16[32,8,8,128]{3,2,1,0:T(8,128)(2,1)} %filter_volumes.1), calls=%async_computation | async-start | bytes 1048576 | tf_op jit(solution)/shard_map/all_to_all | solution.py:307
  30.2 0.8 %copy-start = (bf16[32,8,8,128]{3,2,1,0:T(8,128)(2,1)}, bf16[32,8,8,128]{3,2,1,0:T(8,128)(2,1)S(1)}, u32[]{:S(2)}) copy-start(bf16[32,8,8,128]{3,2,1,0:T(8,128)(2,1)S(1)} %all-to-all-done.received) | copy-start | bytes 1572868
  33.9 1.5 %collective-permute-start = (f32[136,128]{1,0:T(8,128)}, f32[136,128]{1,0:T(8,128)S(1)}, u32[]{:S(2)}, u32[]{:S(2)}) collective-permute-start(f32[136,128]{1,0:T(8,128)} %get-tuple-element.6), channel_id=1, source_target_pairs={{0,1},{1,0},{2,3},{3,2},{4,5},{5,4},{6,7},{7,6},{8,9},{9,8},{10,11... | collective-permute-start | bytes 208904 | tf_op jit(solution)/shard_map/ppermute | solution.py:184
  36.2 5.3 %collective-permute-start.3 = (f32[136,128]{1,0:T(8,128)S(1)}, f32[136,128]{1,0:T(8,128)S(1)}, u32[]{:S(2)}, u32[]{:S(2)}) collective-permute-start(f32[136,128]{1,0:T(8,128)S(1)} %add.27), channel_id=1, source_target_pairs={{0,6},{1,7},{2,4},{3,5},{4,2},{5,3},{6,0},{7,1},{8,14},{9,15},{10,... | collective-permute-start | bytes 208904 | tf_op jit(solution)/shard_map/ppermute | solution.py:184
  38.0 4.9 %collective-permute-start.2 = (f32[136,128]{1,0:T(8,128)S(1)}, f32[136,128]{1,0:T(8,128)S(1)}, u32[]{:S(2)}, u32[]{:S(2)}) collective-permute-start(f32[136,128]{1,0:T(8,128)S(1)} %add.27), channel_id=1, source_target_pairs={{0,4},{1,5},{2,6},{3,7},{4,0},{5,1},{6,2},{7,3},{8,12},{9,13},{10,... | collective-permute-start | bytes 208904 | tf_op jit(solution)/shard_map/ppermute | solution.py:184
  38.6 4.3 %collective-permute-start.1 = (f32[136,128]{1,0:T(8,128)S(1)}, f32[136,128]{1,0:T(8,128)S(1)}, u32[]{:S(2)}, u32[]{:S(2)}) collective-permute-start(f32[136,128]{1,0:T(8,128)S(1)} %add.27), channel_id=1, source_target_pairs={{0,2},{1,3},{2,0},{3,1},{4,6},{5,7},{6,4},{7,5},{8,10},{9,11},{10,... | collective-permute-start | bytes 208904 | tf_op jit(solution)/shard_map/ppermute | solution.py:184
  43.0 4.4 %collective-permute-start.4 = (f32[136,128]{1,0:T(8,128)S(1)}, f32[136,128]{1,0:T(8,128)S(1)}, u32[]{:S(2)}, u32[]{:S(2)}) collective-permute-start(f32[136,128]{1,0:T(8,128)S(1)} %add_add_fusion), channel_id=1, source_target_pairs={{0,8},{1,9},{2,10},{3,11},{4,12},{5,13},{6,14},{7,15},{8,0},{9,1},... | collective-permute-start | bytes 208904 | tf_op jit(solution)/shard_map/ppermute | solution.py:184
  47.3 6.2 %collective-permute-start.5 = (f32[136,128]{1,0:T(8,128)S(1)}, f32[136,128]{1,0:T(8,128)S(1)}, u32[]{:S(2)}, u32[]{:S(2)}) collective-permute-start(f32[136,128]{1,0:T(8,128)S(1)} %add.31), channel_id=1, source_target_pairs={{0,24},{1,25},{2,26},{3,27},{4,28},{5,29},{6,30},{7,31},{8,16},{9,... | collective-permute-start | bytes 208904 | tf_op jit(solution)/shard_map/ppermute | solution.py:184
  53.5 1.3 %copy-start.1 = (f32[136,128]{1,0:T(8,128)}, f32[136,128]{1,0:T(8,128)S(1)}, u32[]{:S(2)}) copy-start(f32[136,128]{1,0:T(8,128)S(1)} %add.32.mine) | copy-start | bytes 208900
  53.5 1.3 %collective-permute-start.6 = (f32[136,128]{1,0:T(8,128)S(1)}, f32[136,128]{1,0:T(8,128)S(1)}, u32[]{:S(2)}, u32[]{:S(2)}) collective-permute-start(f32[136,128]{1,0:T(8,128)S(1)} %add.32.mine), channel_id=1, source_target_pairs={{0,1},{1,0},{2,3},{3,2},{4,5},{5,4},{6,7},{7,6},{8,9},{9,8},{10,11... | collective-permute-start | bytes 208904 | tf_op jit(solution)/shard_map/ppermute | solution.py:184
  54.9 0.6 copy-start.2

commit v3 on v2

--- a/solution.py
+++ b/solution.py
@@ -33,6 +33,13 @@
     return high, low
 
 
+def on_chip(value):
+    return pltpu.with_memory_space_constraint(value, pltpu.VMEM)
+
+
+PARAMS = pltpu.CompilerParams(vmem_limit_bytes=32 << 20)
+
+
 def dot(left, right, contract=((1,), (0,))):
     return lax.dot_general(left, right, (contract, ((), ())), preferred_element_type=jnp.float32)
 
@@ -56,14 +63,15 @@
     return pieces
 
 
-def filter_kernel(frames, row_bands, col_bands, out, held, planes, sems):
+def filter_kernel(frames, row_taps, col_taps, out, held, row_bands, col_bands, planes, sems):
     count, plane_count = frames.shape[0], frames.shape[1]
     half_rows, half_cols = row_bands.shape[0] // 4, col_bands.shape[1] // 2
-    copies = []
-    for t in range(count):
-        copy = pltpu.make_async_copy(frames.at[t], held.at[t], sems.at[t])
+    copies = [pltpu.make_async_copy(frames.at[t], held.at[t], sems.at[t]) for t in range(count)]
+    row_copy = pltpu.make_async_copy(row_taps, row_bands, sems.at[count])
+    col_copy = pltpu.make_async_copy(col_taps, col_bands, sems.at[count + 1])
+    for copy in [row_copy, copies[0], col_copy] + copies[1:]:
         copy.start()
-        copies.append(copy)
+    row_copy.wait()
 
     def row_pass(t):
         copies[t].wait()
@@ -86,6 +94,7 @@
         planes[:, t, :] = wide_sum[:, :half_cols] + (wide_sum[:, half_cols:] + low_sum)
 
     waiting = row_pass(0)
+    col_copy.wait()
     for t in range(count):
         current, waiting = waiting, row_pass(t + 1) if t + 1 < count else None
         column_pass(t, *current)
@@ -108,16 +117,18 @@
     )
     lines = plane_count * (rows // 2)
     shape = (groups, lines // groups, count, cols // 2)
-    vmem = pl.BlockSpec(memory_space=pltpu.VMEM)
+    off_chip = pl.BlockSpec(memory_space=pltpu.HBM)
     return pl.pallas_call(
         filter_kernel,
-        out_shape=jax.ShapeDtypeStruct(shape, jnp.bfloat16),
-        in_specs=[pl.BlockSpec(memory_space=pl.ANY), vmem, vmem],
-        out_specs=vmem,
+        out_shape=pltpu.VMEM(shape, jnp.bfloat16),
+        in_specs=[off_chip] * 3,
+        out_specs=pl.BlockSpec(memory_space=pltpu.VMEM),
         scratch_shapes=[
             pltpu.VMEM(frames.shape, jnp.bfloat16),
+            pltpu.VMEM(row_bands.shape, jnp.bfloat16),
+            pltpu.VMEM(col_bands.shape, jnp.bfloat16),
             pltpu.VMEM((lines, count, cols // 2), jnp.float32),
-            pltpu.SemaphoreType.DMA((count,)),
+            pltpu.SemaphoreType.DMA((count + 2,)),
         ],
         name="filter_volumes",
     )(frames, jnp.asarray(row_bands), jnp.asarray(col_bands))
@@ -170,14 +181,15 @@
     return pl.pallas_call(
         functools.partial(deconvolve_kernel, voxel_count),
         out_shape=(
-            jax.ShapeDtypeStruct((length, lines * width), jnp.bfloat16),
-            jax.ShapeDtypeStruct((length // 2 + SUB, length // 2), jnp.float32),
-            jax.ShapeDtypeStruct((length // 2 + SUB, length // 2), jnp.float32),
+            pltpu.VMEM((length, lines * width), jnp.bfloat16),
+            pltpu.VMEM((length // 2 + SUB, length // 2), jnp.float32),
+            pltpu.VMEM((length // 2 + SUB, length // 2), jnp.float32),
         ),
         in_specs=[pl.BlockSpec(memory_space=pltpu.SMEM), vmem, vmem],
         out_specs=(vmem, vmem, vmem),
+        compiler_params=PARAMS,
         name="deconvolve_gram",
-    )(second, kernel_taps.reshape(1, -1), received)
+    )(second, kernel_taps.reshape(1, -1), on_chip(received))
 
 
 def exchange(value, mask, size):
@@ -297,8 +309,9 @@
         ),
         in_specs=[pl.BlockSpec(memory_space=pltpu.SMEM)] + [vmem] * 4,
         out_specs=(vmem, vmem),
+        compiler_params=PARAMS,
         name="orthonormal_basis",
-    )(second, mine, pairs, sketch, deconvolved)
+    )(second, on_chip(mine), on_chip(pairs), sketch, on_chip(deconvolved))
 
 
 def shards(size, frames, sketch, kernel_taps):

time: 68 us -> 61.5 us (0.904)
  Pallas kernels: 21.6 us -> 17.6 us
  local copies, waits for them, and re-layouts: 1.43 us -> 0.01 us
  other arithmetic: 0.93 us -> 0.05 us
    pallas_call x1, Pallas kernels: 2.84 us -> 0.92 us  [deconvolve_call(): pl.pallas_call(functools.partial(deconvolve_kernel, voxel_count), out_sha...]
    unnamed x6 -> x4, local copies, waits for them, and re-layouts: 1.43 us -> 0.01 us
    pallas_call x1, Pallas kernels: 12.1 us -> 11 us  [basis_call(): pl.pallas_call(basis_kernel, out_shape=(jax.ShapeDtypeStruct((rank, decon...]
    pallas_call x1, Pallas kernels: 6.62 us -> 5.73 us  [filter_call(): pl.pallas_call(filter_kernel, out_shape=pltpu.VMEM(shape, jnp.bfloat16),...]
    add x1, other arithmetic: 0.89 us -> 0.01 us  [sum_over_devices(): half = keep + exchange(send, 1, size)]
where the time goes in v3:
time: 61.5 us; the launch traced here: 61.2 us
  waiting for transfers between devices  29.5 us (48%)
  Pallas kernels  17.6 us (29%)
  starting transfers between devices  13.3 us (22%)
  between operations  0.72 us (1%)
    all_to_all x1, waiting for transfers between devices, shards(): lax.all_to_all(filtered, AXES, split_axis=0, concat_axis=0, tiled=True)  15.6 us
    ppermute x7, waiting for transfers between devices, exchange(): return lax.ppermute(value, AXES, [(i, i ^ mask) for i in range(size)])  13.9 us
    pallas_call x1, Pallas kernels, basis_call(): pl.pallas_call(basis_kernel, out_shape=(jax.ShapeDtypeStruct((rank, decon...  11 us
    all_to_all x1, starting transfers between devices, shards(): lax.all_to_all(filtered, AXES, split_axis=0, concat_axis=0, tiled=True)  7.33 us
    ppermute x7, starting transfers between devices, exchange(): return lax.ppermute(value, AXES, [(i, i ^ mask) for i in range(size)])  5.99 us
    pallas_call x1, Pallas kernels, filter_call(): pl.pallas_call(filter_kernel, out_shape=pltpu.VMEM(shape, jnp.bfloat16),...  5.73 us
  transfers between devices with their start and end apart: 8, of which 7 were waited for; matrix products, arithmetic and copies ran while one was open for 0% of the time, Pallas kernels for 0%

profile of v3, /device:TPU:0, one launch (start us, length us, event | category | flops | bytes accessed | tf_op | source)
XLA Modules:
  0.0 61.2 jit_solution(16832518944325274)
XLA Ops:
  0.6 0.0 copy-start.1
  0.6 0.0 copy-start
  0.6 5.7 %filter_volumes.1 = bf16[32,8,8,128]{3,2,1,0:T(8,128)(2,1)} custom-call(bf16[8,2,256,256]{3,2,1,0:T(8,128)(2,1)} %frames.1, bf16[512,256]{1,0:T(8,128)(2,1)} %constant.28.clone.row_taps, bf16[512,256]{1,0:T(8,128)(2,1)} %constant.29.clone.col_taps), custom_call_target="tpu_custom_call" | custom-call | tf_op jit(solution)/shard_map/filter_volumes/pallas_call | solution.py:121
  6.4 7.3 %all-to-all-start = ((bf16[32,8,8,128]{3,2,1,0:T(8,128)(2,1)}), bf16[32,8,8,128]{3,2,1,0:T(8,128)(2,1)S(1)}, u32[]{:S(2)}, u32[]{:S(2)}) async-start(bf16[32,8,8,128]{3,2,1,0:T(8,128)(2,1)} %filter_volumes.1), calls=%async_computation | async-start | bytes 1048576 | tf_op jit(solution)/shard_map/all_to_all | solution.py:320
  13.7 15.6 %all-to-all-done.received = bf16[32,8,8,128]{3,2,1,0:T(8,128)(2,1)S(1)} async-done(((bf16[32,8,8,128]{3,2,1,0:T(8,128)(2,1)}), bf16[32,8,8,128]{3,2,1,0:T(8,128)(2,1)S(1)}, u32[]{:S(2)}, u32[]{:S(2)}) %all-to-all-start) | async-done | bytes 524320 | tf_op jit(solution)/shard_map/all_to_all | solution.py:320
  29.3 0.0 copy-done.1
  29.3 0.9 %deconvolve_gram.1 = (bf16[256,1024]{1,0:T(8,128)(2,1)S(1)}, f32[136,128]{1,0:T(8,128)S(1)}, f32[136,128]{1,0:T(8,128)S(1)}) custom-call(s32[1]{0:T(128)} %bitcast.second, bf16[1,64]{1,0:T(2,128)(2,1)S(1)} %bitcast.2, bf16[32,8,8,128]{3,2,1,0:T(8,128)(2,1)S(1)} %all-to-all-done.received), custom_call_target="tpu_custom_call" | custom-call | tf_op jit(solution)/shard_map/deconvolve_gram/pallas_call | solution.py:181
  30.3 0.1 collective-permute-start
  30.3 1.2 %collective-permute-done = f32[136,128]{1,0:T(8,128)S(1)} collective-permute-done((f32[136,128]{1,0:T(8,128)S(1)}, f32[136,128]{1,0:T(8,128)S(1)}, u32[]{:S(2)}, u32[]{:S(2)}) %collective-permute-start) | collective-permute-done | bytes 69664 | tf_op jit(solution)/shard_map/ppermute | solution.py:196
  31.6 1.8 %collective-permute-start.3 = (f32[136,128]{1,0:T(8,128)S(1)}, f32[136,128]{1,0:T(8,128)S(1)}, u32[]{:S(2)}, u32[]{:S(2)}) collective-permute-start(f32[136,128]{1,0:T(8,128)S(1)} %add.27), channel_id=1, source_target_pairs={{0,6},{1,7},{2,4},{3,5},{4,2},{5,3},{6,0},{7,1},{8,14},{9,15},{10,... | collective-permute-start | bytes 208904 | tf_op jit(solution)/shard_map/ppermute | solution.py:196
  33.4 0.6 collective-permute-start.2
  34.0 1.2 %collective-permute-start.1 = (f32[136,128]{1,0:T(8,128)S(1)}, f32[136,128]{1,0:T(8,128)S(1)}, u32[]{:S(2)}, u32[]{:S(2)}) collective-permute-start(f32[136,128]{1,0:T(8,128)S(1)} %add.27), channel_id=1, source_target_pairs={{0,2},{1,3},{2,0},{3,1},{4,6},{5,7},{6,4},{7,5},{8,10},{9,11},{10,... | collective-permute-start | bytes 208904 | tf_op jit(solution)/shard_map/ppermute | solution.py:196
  35.2 1.8 %collective-permute-done.3 = f32[136,128]{1,0:T(8,128)S(1)} collective-permute-done((f32[136,128]{1,0:T(8,128)S(1)}, f32[136,128]{1,0:T(8,128)S(1)}, u32[]{:S(2)}, u32[]{:S(2)}) %collective-permute-start.3) | collective-permute-done | bytes 69664 | tf_op jit(solution)/shard_map/ppermute | solution.py:196
  36.9 1.4 %collective-permute-done.2 = f32[136,128]{1,0:T(8,128)S(1)} collective-permute-done((f32[136,128]{1,0:T(8,128)S(1)}, f32[136,128]{1,0:T(8,128)S(1)}, u32[]{:S(2)}, u32[]{:S(2)}) %collective-permute-start.2) | collective-permute-done | bytes 69664 | tf_op jit(solution)/shard_map/ppermute | solution.py:196
  38.3 0.0 collective-permute-done.1
  38.3 0.8 %collective-permute-start.4 = (f32[136,128]{1,0:T(8,128)S(1)}, f32[136,128]{1,0:T(8,128)S(1)}, u32[]{:S(2)}, u32[]{:S(2)}) collective-permute-start(f32[136,128]{1,0:T(8,128)S(1)} %add_add_fusion), channel_id=1, source_target_pairs={{0,8},{1,9},{2,10},{3,11},{4,12},{5,13},{6,14},{7,15},{8,0},{9,1},... | collective-permute-start | bytes 208904 | tf_op jit(solution)/shard_map/ppermute | solution.py:196
  39.2 3.5 %collective-permute-done.4 = f32[136,128]{1,0:T(8,128)S(1)} collective-permute-done((f32[136,128]{1,0:T(8,128)S(1)}, f32[136,128]{1,0:T(8,128)S(1)}, u32[]{:S(2)}, u32[]{:S(2)}) %collective-permute-start.4) | collective-permute-done | bytes 69664 | tf_op jit(solution)/shard_map/ppermute | solution.py:196
  42.7 1.5 %collective-permute-start.5 = (f32[136,128]{1,0:T(8,128)S(1)}, f32[136,128]{1,0:T(8,128)S(1)}, u32[]{:S(2)}, u32[]{:S(2)}) collective-permute-start(f32[136,128]{1,0:T(8,128)S(1)} %add.31), channel_id=1, source_target_pairs={{0,24},{1,25},{2,26},{3,27},{4,28},{5,29},{6,30},{7,31},{8,16},{9,... | collective-permute-start | bytes 208904 | tf_op jit(solution)/shard_map/ppermute | solution.py:196
  44.2 4.7 %collective-permute-done.5 = f32[136,128]{1,0:T(8,128)S(1)} collective-permute-done((f32[136,128]{1,0:T(8,128)S(1)}, f32[136,128]{1,0:T(8,128)S(1)}, u32[]{:S(2)}, u32[]{:S(2)}) %collective-permute-start.5) | collective-permute-done | bytes 69664 | tf_op jit(solution)/shard_map/ppermute | solution.py:196
  48.9 0.1 collective-permute-start.6
  49.0 1.2 %collective-permute-done.6.pairs = f32[136,128]{1,0:T(8,128)S(1)} collective-permute-done((f32[136,128]{1,0:T(8,128)S(1)}, f32[136,128]{1,0:T(8,128)S(1)}, u32[]{:S(2)}, u32[]{:S(2)}) %collective-permute-start.6) | collective-permute-done | bytes 69664 | tf_op jit(solution)/shard_map/ppermute | solution.py:196
  50.2 0.0 copy-done
  50.2 11.0 %orthonormal_basis.1 = (f32[128,1024]{1,0:T(8,128)}, f32[128,128]{1,0:T(8,128)}) custom-call(s32[1]{0:T(128)} %bitcast.second, f32[136,128]{1,0:T(8,128)S(1)} %add.32.mine, f32[136,128]{1,0:T(8,128)S(1)} %collective-permute-done.6.pairs, bf16[256,128]{1,0:T(8,128)(2,1)S(1)} %copy-done, bf16[256,1024]{1,0:T(8,128)(2,1)S(1)} %get-tuple-element.7.deconvolved), custom_call_target="tpu_custom_call" | custom-call | tf_op jit(solution)/shard_map/orthonormal_basis/pallas_call | solution.py:304
  (4 shorter events, 0.0 us)
Async XLA Ops:
  0.6 28.7 %copy-start.1 = (bf16[64]{0:T(256)(128)(2,1)S(1)}, bf16[64]{0:T(256)(128)(2,1)}, u32[]{:S(2)}) copy-start(bf16[64]{0:T(256)(128)(2,1)} %param.7) | copy-start | bytes 388
  0.6 49.6 %copy-start = (bf16[256,128]{1,0:T(8,128)(2,1)S(1)}, bf16[256,128]{1,0:T(8,128)(2,1)}, u32[]{:S(2)}) copy-start(bf16[256,128]{1,0:T(8,128)(2,1)} %sketch.1) | copy-start | bytes 196612
  6.4 23.0 %all-to-all-start = ((bf16[32,8,8,128]{3,2,1,0:T(8,128)(2,1)}), bf16[32,8,8,128]{3,2,1,0:T(8,128)(2,1)S(1)}, u32[]{:S(2)}, u32[]{:S(2)}) async-start(bf16[32,8,8,128]{3,2,1,0:T(8,128)(2,1)} %filter_volumes.1), calls=%async_computation | async-start | bytes 1048576 | tf_op jit(solution)/shard_map/all_to_all | solution.py:320
  30.3 1.3 %collective-permute-start = (f32[136,128]{1,0:T(8,128)S(1)}, f32[136,128]{1,0:T(8,128)S(1)}, u32[]{:S(2)}, u32[]{:S(2)}) collective-permute-start(f32[136,128]{1,0:T(8,128)S(1)} %get-tuple-element.6), channel_id=1, source_target_pairs={{0,1},{1,0},{2,3},{3,2},{4,5},{5,4},{6,7},{7,6},{8,9},{9,8},{10,11... | collective-permute-start | bytes 208904 | tf_op jit(solution)/shard_map/ppermute | solution.py:196
  31.6 5.3 %collective-permute-start.3 = (f32[136,128]{1,0:T(8,128)S(1)}, f32[136,128]{1,0:T(8,128)S(1)}, u32[]{:S(2)}, u32[]{:S(2)}) collective-permute-start(f32[136,128]{1,0:T(8,128)S(1)} %add.27), channel_id=1, source_target_pairs={{0,6},{1,7},{2,4},{3,5},{4,2},{5,3},{6,0},{7,1},{8,14},{9,15},{10,... | collective-permute-start | bytes 208904 | tf_op jit(solution)/shard_map/ppermute | solution.py:196
  33.4 4.9 %collective-permute-start.2 = (f32[136,128]{1,0:T(8,128)S(1)}, f32[136,128]{1,0:T(8,128)S(1)}, u32[]{:S(2)}, u32[]{:S(2)}) collective-permute-start(f32[136,128]{1,0:T(8,128)S(1)} %add.27), channel_id=1, source_target_pairs={{0,4},{1,5},{2,6},{3,7},{4,0},{5,1},{6,2},{7,3},{8,12},{9,13},{10,... | collective-permute-start | bytes 208904 | tf_op jit(solution)/shard_map/ppermute | solution.py:196
  34.0 4.3 %collective-permute-start.1 = (f32[136,128]{1,0:T(8,128)S(1)}, f32[136,128]{1,0:T(8,128)S(1)}, u32[]{:S(2)}, u32[]{:S(2)}) collective-permute-start(f32[136,128]{1,0:T(8,128)S(1)} %add.27), channel_id=1, source_target_pairs={{0,2},{1,3},{2,0},{3,1},{4,6},{5,7},{6,4},{7,5},{8,10},{9,11},{10,... | collective-permute-start | bytes 208904 | tf_op jit(solution)/shard_map/ppermute | solution.py:196
  38.3 4.4 %collective-permute-start.4 = (f32[136,128]{1,0:T(8,128)S(1)}, f32[136,128]{1,0:T(8,128)S(1)}, u32[]{:S(2)}, u32[]{:S(2)}) collective-permute-start(f32[136,128]{1,0:T(8,128)S(1)} %add_add_fusion), channel_id=1, source_target_pairs={{0,8},{1,9},{2,10},{3,11},{4,12},{5,13},{6,14},{7,15},{8,0},{9,1},... | collective-permute-start | bytes 208904 | tf_op jit(solution)/shard_map/ppermute | solution.py:196
  42.7 6.2 %collective-permute-start.5 = (f32[136,128]{1,0:T(8,128)S(1)}, f32[136,128]{1,0:T(8,128)S(1)}, u32[]{:S(2)}, u32[]{:S(2)}) collective-permute-start(f32[136,128]{1,0:T(8,128)S(1)} %add.31), channel_id=1, source_target_pairs={{0,24},{1,25},{2,26},{3,27},{4,28},{5,29},{6,30},{7,31},{8,16},{9,... | collective-permute-start | bytes 208904 | tf_op jit(solution)/shard_map/ppermute | solution.py:196
  48.9 1.3 %collective-permute-start.6 = (f32[136,128]{1,0:T(8,128)S(1)}, f32[136,128]{1,0:T(8,128)S(1)}, u32[]{:S(2)}, u32[]{:S(2)}) collective-permute-start(f32[136,128]{1,0:T(8,128)S(1)} %add.32.mine), channel_id=1, source_target_pairs={{0,1},{1,0},{2,3},{3,2},{4,5},{5,4},{6,7},{7,6},{8,9},{9,8},{10,11... | collective-permute-start | bytes 208904 | tf_op jit(solution)/shard_map/ppermute | solution.py:196
